TPU v7x, 512 devices: a whole 4x8x8 slice. The times are simulated.
512 devices in a mesh: dp: 8 (over z), expert: 64 (over x, y, core).
Axes of the slice: x: 4, y: 8, z: 8, core: 2. Of those that a mesh axis runs over, the one named last changes fastest.
Arguments:
- tokens: bfloat16 [65536, 1024], P(('dp', 'expert')), may hold values from -6 to 6
- d_output: bfloat16 [65536, 1024], P(('dp', 'expert')), may hold values from -6 to 6
- combine: float32 [65536, 8], P(('dp', 'expert')), may hold values from 0.05 to 1
- routes: int32 [65536, 8], P(('dp', 'expert')), may hold values from 0 to 63, all different within a row; in each aligned block of 128 rows (0 to 127, 128 to 255, ...) at most 18 rows name the same one
- gate_weight: bfloat16 [64, 1024, 384], P('expert', 'dp'), may hold values from -0.1875 to 0.1875
- up_weight: bfloat16 [64, 1024, 384], P('expert', 'dp'), may hold values from -0.1875 to 0.1875
- down_weight: bfloat16 [64, 384, 1024], P('expert', None, 'dp'), may hold values from -0.3125 to 0.3125
Outputs:
- d_tokens: bfloat16 [65536, 1024], P(('dp', 'expert'))
- d_gate_weight: float32 [64, 1024, 384], P('expert', 'dp')
- d_up_weight: float32 [64, 1024, 384], P('expert', 'dp')
- d_down_weight: float32 [64, 384, 1024], P('expert', None, 'dp')
Inputs may be any that keep to these rules, and one draw needn't show every extreme that they name: `routes`: among the 128 tokens of one device, each expert id is named by at most 18 rows; some expert is named by exactly 18 rows on some device. The ids of one token differ.
All inputs are finite; a program needn't handle non-finite values.
Results may differ from a plain program's by a relative error of at most 0.015.
Values may be sent and summed in bfloat16 or wider, within the bound.
A program may use at most 64 MiB of HBM per device.

v0:
```python
import jax
import jax.numpy as jnp
from jax import lax
from jax.sharding import PartitionSpec as P


def route_slots(routes, experts):
    matches = (routes[:, :, None] == jnp.arange(experts, dtype=jnp.int32)[None, None, :]).astype(
        jnp.int32
    )
    per_token = jnp.sum(matches, axis=1)
    tok_count = per_token.shape[0]
    before = jnp.tri(tok_count, k=-1, dtype=jnp.bfloat16)
    earlier = jnp.dot(
        before, per_token.astype(jnp.bfloat16), preferred_element_type=jnp.float32
    ).astype(jnp.int32)
    return jnp.sum(matches * earlier[:, None, :], axis=2)


def row_work(row_inputs, row_grads, gate_up, down_matrix):
    hidden_units = down_matrix.shape[0]
    preact = jnp.dot(row_inputs, gate_up, preferred_element_type=jnp.float32)
    gate_pre = preact[:, :hidden_units]
    up_pre = preact[:, hidden_units:]
    gate_sigmoid = jax.nn.sigmoid(gate_pre)
    hidden = (gate_pre * gate_sigmoid * up_pre).astype(jnp.bfloat16)
    d_hidden = jnp.dot(row_grads, down_matrix.T, preferred_element_type=jnp.float32)
    d_gate_pre = d_hidden * up_pre * gate_sigmoid * (1.0 + gate_pre * (1.0 - gate_sigmoid))
    d_up_pre = d_hidden * gate_pre * gate_sigmoid
    d_preact = jnp.concatenate([d_gate_pre, d_up_pre], axis=1).astype(jnp.bfloat16)
    d_rows = jnp.dot(d_preact, gate_up.T, preferred_element_type=jnp.float32).astype(jnp.bfloat16)
    return (d_rows, hidden, d_preact)


def body(tokens, d_output, combine, routes, gate_weight, up_weight, down_weight):
    experts = lax.axis_size("expert")
    tok_count = tokens.shape[0]
    model_width = tokens.shape[1]
    top_count = routes.shape[1]
    capacity = max(2, (9 * tok_count * top_count + 8 * experts - 1) // (8 * experts))
    slot_count = experts * capacity
    slot_index = route_slots(routes, experts)
    position = (routes * capacity + slot_index).reshape(-1)
    spread_inputs = jnp.repeat(tokens, top_count, axis=0)
    scaled = (
        (combine[:, :, None] * d_output[:, None, :].astype(jnp.float32))
        .astype(jnp.bfloat16)
        .reshape(-1, model_width)
    )
    send_inputs = (
        jnp.zeros((slot_count, model_width), jnp.bfloat16)
        .at[position]
        .set(spread_inputs)
        .reshape(experts, capacity, model_width)
    )
    send_grads = (
        jnp.zeros((slot_count, model_width), jnp.bfloat16)
        .at[position]
        .set(scaled)
        .reshape(experts, capacity, model_width)
    )
    whole_gate, whole_up, whole_down = (
        lax.all_gather(gate_weight, "dp", axis=1, tiled=True),
        lax.all_gather(up_weight, "dp", axis=1, tiled=True),
        lax.all_gather(down_weight, "dp", axis=2, tiled=True),
    )
    gate_up = jnp.concatenate([whole_gate[0], whole_up[0]], axis=1)
    down_matrix = whole_down[0]
    hidden_units = down_matrix.shape[0]
    recv_inputs, recv_grads = (
        lax.all_to_all(send_inputs, "expert", split_axis=0, concat_axis=0, tiled=True),
        lax.all_to_all(send_grads, "expert", split_axis=0, concat_axis=0, tiled=True),
    )
    flat_inputs = recv_inputs.reshape(-1, model_width)
    flat_grads = recv_grads.reshape(-1, model_width)
    d_rows, hidden, d_preact = row_work(flat_inputs, flat_grads, gate_up, down_matrix)
    returned = lax.all_to_all(
        d_rows.reshape(experts, capacity, model_width),
        "expert",
        split_axis=0,
        concat_axis=0,
        tiled=True,
    )
    route_rows = returned.reshape(-1, model_width)[position].reshape(
        tok_count, top_count, model_width
    )
    d_tokens = jnp.sum(route_rows.astype(jnp.float32), axis=1).astype(jnp.bfloat16)
    gate_up_grad = jnp.dot(flat_inputs.T, d_preact, preferred_element_type=jnp.float32)
    down_grad = jnp.dot(flat_grads.T, hidden, preferred_element_type=jnp.float32)
    stacked = jnp.concatenate([gate_up_grad, down_grad], axis=1)
    summed = lax.psum_scatter(
        stacked.astype(jnp.bfloat16), "dp", scatter_dimension=0, tiled=True
    ).astype(jnp.float32)
    d_gate_weight = summed[:, :hidden_units][None]
    d_up_weight = summed[:, hidden_units : 2 * hidden_units][None]
    d_down_weight = summed[:, 2 * hidden_units :].T[None]
    return (d_tokens, d_gate_weight, d_up_weight, d_down_weight)


def solution(mesh):
    placed = (
        P(("dp", "expert"), None),
        P(("dp", "expert"), None),
        P(("dp", "expert"), None),
        P(("dp", "expert"), None),
        P("expert", "dp", None),
        P("expert", "dp", None),
        P("expert", None, "dp"),
    )
    return jax.shard_map(
        body,
        mesh=mesh,
        in_specs=placed,
        out_specs=(
            P(("dp", "expert"), None),
            P("expert", "dp", None),
            P("expert", "dp", None),
            P("expert", None, "dp"),
        ),
        check_vma=False,
    )
```

profile of v0, /device:TPU:1, one launch (start us, length us, event | category | flops | bytes accessed | tf_op | source)
XLA Modules:
  0.0 330.3 jit_solution(3674698657693354905)
XLA Ops:
  9.8 6.0 %scatter_custom_fusion.1 = bf16[1152,1024]{1,0:T(8,128)(2,1)S(1)} fusion(s32[1024]{0:T(1024)S(1)} %bitcast.37, bf16[]{:T(256)} %constant.6.clone.1, bf16[128,1024]{1,0:T(8,128)(2,1)S(1)} %copy-done), kind=kCustom, calls=%fused_computation.9 | custom fusion | bytes 2621442 | tf_op jit(solution)/shard_map/scatter | solution.py:53
  15.9 2.4 reshape.76
  18.3 11.8 %all-to-all-start.1 = ((bf16[64,18,1024]{2,1,0:T(8,128)(2,1)}), bf16[64,18,1024]{2,1,0:T(8,128)(2,1)S(1)}, u32[]{:S(2)}, u32[]{:S(2)}) async-start(bf16[64,18,1024]{2,1,0:T(8,128)(2,1)} %reshape.76), calls=%async_computation.1 | async-start | bytes 6291456 | tf_op jit(solution)/shard_map/all_to_all | solution.py:71
  30.2 1.8 convert_element_type.34
  32.0 7.7 %scatter_custom_fusion = bf16[1152,1024]{1,0:T(8,128)(2,1)} fusion(s32[1024]{0:T(1024)S(1)} %bitcast.38, f32[128,1024]{1,0:T(8,128)} %convert_element_type.34, f32[1024]{0:T(1024)S(1)} %mul.60, bf16[]{:T(256)} %constant.6.clone.1), kind=kCustom, calls=%fused_computation.7 | custom fusion | flops 2097152 | bytes 2887682 | tf_op jit(solution)/shard_map/scatter | solution.py:59
  39.7 4.3 %reshape.73 = bf16[64,18,1024]{2,1,0:T(8,128)(2,1)} reshape(bf16[1152,1024]{1,0:T(8,128)(2,1)} %scatter_custom_fusion) | data formatting | bytes 4718592 | tf_op jit(solution)/shard_map/reshape | solution.py:60
  44.1 59.5 %all-to-all-done.1 = bf16[64,18,1024]{2,1,0:T(8,128)(2,1)S(1)} async-done(((bf16[64,18,1024]{2,1,0:T(8,128)(2,1)}), bf16[64,18,1024]{2,1,0:T(8,128)(2,1)S(1)}, u32[]{:S(2)}, u32[]{:S(2)}) %all-to-all-start.1) | async-done | bytes 2359328 | tf_op jit(solution)/shard_map/all_to_all | solution.py:71
  103.5 6.2 %all-to-all-start = ((bf16[64,18,1024]{2,1,0:T(8,128)(2,1)}), bf16[64,18,1024]{2,1,0:T(8,128)(2,1)}, u32[]{:S(2)}, u32[]{:S(2)}) async-start(bf16[64,18,1024]{2,1,0:T(8,128)(2,1)} %reshape.73), calls=%async_computation | async-start | bytes 6291456 | tf_op jit(solution)/shard_map/all_to_all | solution.py:72
  109.8 30.3 %all_gather.10 = bf16[1,1024,384]{2,1,0:T(8,128)(2,1)} all-gather(bf16[1,128,384]{2,1,0:T(8,128)(2,1)S(1)} %copy-done.5), channel_id=1, replica_groups=mesh['dp'=8,'expert'=64] {'dp'}, dimensions={1}, use_global_device_ids=true | all-gather | bytes 884736 | tf_op jit(solution)/shard_map/all_gather | solution.py:63
  140.1 24.1 %all_gather.11 = bf16[1,1024,384]{2,1,0:T(8,128)(2,1)} all-gather(bf16[1,128,384]{2,1,0:T(8,128)(2,1)} %param.12), channel_id=1, replica_groups=mesh['dp'=8,'expert'=64] {'dp'}, dimensions={1}, use_global_device_ids=true | all-gather | bytes 884736 | tf_op jit(solution)/shard_map/all_gather | solution.py:64
  164.2 22.5 %all_gather.9 = bf16[1,384,1024]{2,1,0:T(8,128)(2,1)} all-gather(bf16[1,384,128]{2,1,0:T(8,128)(2,1)} %param.13), channel_id=1, replica_groups=mesh['dp'=8,'expert'=64] {'dp'}, dimensions={2}, use_global_device_ids=true | all-gather | bytes 884736 | tf_op jit(solution)/shard_map/all_gather | solution.py:65
  186.7 2.2 reshape.77
  188.9 6.1 %fusion.10 = f32[1152,768]{0,1:T(8,128)} fusion(bf16[1152,1024]{1,0:T(8,128)(2,1)} %reshape.77, bf16[1024,384]{1,0:T(8,128)(2,1)} %bitcast.35, bf16[1024,384]{1,0:T(8,128)(2,1)} %bitcast.33), kind=kOutput, calls=%fused_computation.25 | convolution fusion | flops 1815085056 | bytes 7471104 | tf_op jit(solution)/shard_map/dot_general | solution.py:22
  195.0 2.9 reshape.74
  197.9 3.4 %convolution_convert_fusion.2 = bf16[1024,384]{0,1:T(8,128)(2,1)S(1)} fusion(bf16[1152,1024]{1,0:T(8,128)(2,1)S(1)} %reshape.74, f32[1152,768]{0,1:T(8,128)} %fusion.10), kind=kOutput, calls=%fused_computation.20 | convolution fusion | flops 909017088 | bytes 6684672 | tf_op jit(solution)/shard_map/dot_general | solution.py:89
  203.0 3.3 %convolution_convert_fusion.1 = bf16[1024,768]{0,1:T(8,128)(2,1)} fusion(bf16[1152,1024]{1,0:T(8,128)(2,1)S(1)} %copy-done.1, bf16[1152,384]{0,1:T(8,128)(2,1)S(1)} %get-tuple-element.21, bf16[1152,384]{0,1:T(8,128)(2,1)S(1)} %get-tuple-element.20), kind=kOutput, calls=%fused_computation.18 | convolution fusion | flops 1816264704 | bytes 5701632 | tf_op jit(solution)/shard_map/dot_general | solution.py:88
  206.4 2.1 convolution_convert_fusion
  208.5 2.4 reshape.78
  210.9 23.6 %all-to-all-start.2 = ((bf16[64,18,1024]{2,1,0:T(8,128)(2,1)}), bf16[64,18,1024]{2,1,0:T(8,128)(2,1)}, u32[]{:S(2)}, u32[]{:S(2)}) async-start(bf16[64,18,1024]{2,1,0:T(8,128)(2,1)} %reshape.78), calls=%async_computation.2 | async-start | bytes 6291456 | tf_op jit(solution)/shard_map/all_to_all | solution.py:77
  236.4 2.6 copy.31
  239.0 68.9 %all-to-all-done.2 = bf16[64,18,1024]{2,1,0:T(8,128)(2,1)} async-done(((bf16[64,18,1024]{2,1,0:T(8,128)(2,1)}), bf16[64,18,1024]{2,1,0:T(8,128)(2,1)}, u32[]{:S(2)}, u32[]{:S(2)}) %all-to-all-start.2) | async-done | bytes 2359328 | tf_op jit(solution)/shard_map/all_to_all | solution.py:77
  307.9 2.9 reshape.79
  310.9 5.3 %gather_fusion = bf16[1024,1024]{1,0:T(8,128)(2,1)} fusion(bf16[1152,1024]{1,0:T(8,128)(2,1)S(1)} %reshape.79, s32[1024]{0:T(1024)S(1)} %broadcast_clamp_fusion), kind=kCustom, calls=%fused_computation | custom fusion | bytes 4198400 | tf_op jit(solution)/shard_map/gather | solution.py:84
  316.2 3.7 %bitcast_reduce_fusion = bf16[128,1024]{1,0:T(8,128)(2,1)} fusion(bf16[1024,1024]{1,0:T(8,128)(2,1)} %gather_fusion), kind=kLoop, calls=%fused_computation.8 | loop fusion | flops 917504 | bytes 2359296 | tf_op jit(solution)/shard_map/reduce_sum | solution.py:87
  (38 shorter events, 9.9 us)
Async XLA Ops:
  7.2 2.7 copy-start
  18.3 11.8 %copy-start.6 = (f32[128,8]{0,1:T(8,128)S(1)}, f32[128,8]{0,1:T(8,128)}, u32[]{:S(2)}) copy-start(f32[128,8]{0,1:T(8,128)} %param.9) | copy-start | bytes 12292
  18.3 85.3 %all-to-all-start.1 = ((bf16[64,18,1024]{2,1,0:T(8,128)(2,1)}), bf16[64,18,1024]{2,1,0:T(8,128)(2,1)S(1)}, u32[]{:S(2)}, u32[]{:S(2)}) async-start(bf16[64,18,1024]{2,1,0:T(8,128)(2,1)} %reshape.76), calls=%async_computation.1 | async-start | bytes 6291456 | tf_op jit(solution)/shard_map/all_to_all | solution.py:71
  44.1 65.7 %copy-start.5 = (bf16[1,128,384]{2,1,0:T(8,128)(2,1)S(1)}, bf16[1,128,384]{2,1,0:T(8,128)(2,1)}, u32[]{:S(2)}) copy-start(bf16[1,128,384]{2,1,0:T(8,128)(2,1)} %param.11) | copy-start | bytes 294916
  103.5 91.4 %all-to-all-start = ((bf16[64,18,1024]{2,1,0:T(8,128)(2,1)}), bf16[64,18,1024]{2,1,0:T(8,128)(2,1)}, u32[]{:S(2)}, u32[]{:S(2)}) async-start(bf16[64,18,1024]{2,1,0:T(8,128)(2,1)} %reshape.73), calls=%async_computation | async-start | bytes 6291456 | tf_op jit(solution)/shard_map/all_to_all | solution.py:72
  197.9 3.4 %copy-start.4 = (bf16[1,384,1024]{2,1,0:T(8,128)(2,1)S(1)}, bf16[1,384,1024]{2,1,0:T(8,128)(2,1)}, u32[]{:S(2)}) copy-start(bf16[1,384,1024]{2,1,0:T(8,128)(2,1)} %all_gather.9) | copy-start | bytes 2359300
  197.9 3.4 %copy-start.7 = (f32[1152,768]{0,1:T(8,128)S(1)}, f32[1152,768]{0,1:T(8,128)}, u32[]{:S(2)}) copy-start(f32[1152,768]{0,1:T(8,128)} %fusion.10) | copy-start | bytes 10616836
  201.4 1.7 copy-start.1
  203.0 3.4 %copy-start.2 = (bf16[1,1024,384]{2,1,0:T(8,128)(2,1)S(1)}, bf16[1,1024,384]{2,1,0:T(8,128)(2,1)}, u32[]{:S(2)}) copy-start(bf16[1,1024,384]{2,1,0:T(8,128)(2,1)} %all_gather.10) | copy-start | bytes 2359300
  203.0 3.4 %copy-start.3 = (bf16[1,1024,384]{2,1,0:T(8,128)(2,1)S(1)}, bf16[1,1024,384]{2,1,0:T(8,128)(2,1)}, u32[]{:S(2)}) copy-start(bf16[1,1024,384]{2,1,0:T(8,128)(2,1)} %all_gather.11) | copy-start | bytes 2359300
  210.9 97.1 %all-to-all-start.2 = ((bf16[64,18,1024]{2,1,0:T(8,128)(2,1)}), bf16[64,18,1024]{2,1,0:T(8,128)(2,1)}, u32[]{:S(2)}, u32[]{:S(2)}) async-start(bf16[64,18,1024]{2,1,0:T(8,128)(2,1)} %reshape.78), calls=%async_computation.2 | async-start | bytes 6291456 | tf_op jit(solution)/shard_map/all_to_all | solution.py:77
  234.5 85.5 %reduce-scatter.4.cloned.1.call-start = ((), (), s32[]{:S(2)}) async-start(), calls=%async_computation.4 | async-start | bytes 2654208
Sparse Core Ops, SparseCore 0:
  239.1 41.3 reduce-scatter.3
where the time goes:
time: 331 us; the launch traced here: 330 us
  waiting for transfers between devices  128 us (39%)
  blocking collectives  76.9 us (23%)
  starting transfers between devices  41.9 us (13%)
  local copies, waits for them, and re-layouts  35.2 us (11%)
  other arithmetic  17.1 us (5%)
  matrix products  16.7 us (5%)
  between operations  14.2 us (4%)
    all_to_all x1, waiting for transfers between devices, body(): lax.all_to_all(d_rows.reshape(experts, capacity, model_width), 'expert',...  68.9 us
    all_to_all x1, waiting for transfers between devices, body(): lax.all_to_all(send_inputs, 'expert', split_axis=0, concat_axis=0, tiled=...  59.5 us
    all_gather x1, blocking collectives, body(): lax.all_gather(gate_weight, 'dp', axis=1, tiled=True)  30.3 us
    all_gather x1, blocking collectives, body(): lax.all_gather(up_weight, 'dp', axis=1, tiled=True)  24.1 us
    all_to_all x1, starting transfers between devices, body(): lax.all_to_all(d_rows.reshape(experts, capacity, model_width), 'expert',...  23.6 us
    all_gather x1, blocking collectives, body(): lax.all_gather(down_weight, 'dp', axis=2, tiled=True)  22.5 us
    all_to_all x1, starting transfers between devices, body(): lax.all_to_all(send_inputs, 'expert', split_axis=0, concat_axis=0, tiled=...  11.8 us
    scatter x1, other arithmetic, body(): send_grads = jnp.zeros((slot_count, model_width), jnp.bfloat16).at[positi...  7.72 us
  transfers between devices with their start and end apart: 4, of which 2 were waited for; matrix products, arithmetic and copies ran while one was open for 12% of the time, Pallas kernels for 0%

commit v1 on v0

--- a/solution.py
+++ b/solution.py
@@ -62,7 +62,9 @@
     whole_gate, whole_up, whole_down = (
         lax.all_gather(gate_weight, "dp", axis=1, tiled=True),
         lax.all_gather(up_weight, "dp", axis=1, tiled=True),
-        lax.all_gather(down_weight, "dp", axis=2, tiled=True),
+        jnp.concatenate(
+            lax.all_to_all(jnp.stack([down_weight] * lax.axis_size("dp")), "dp", 0, 0), axis=2
+        ),
     )
     gate_up = jnp.concatenate([whole_gate[0], whole_up[0]], axis=1)
     down_matrix = whole_down[0]

time: 331 us -> 395 us (1.19)
  waiting for transfers between devices: 128 us -> 204 us
  blocking collectives: 76.9 us -> 60.8 us
  local copies, waits for them, and re-layouts: 35.2 us -> 40.6 us
    all_to_all x1, waiting for transfers between devices: 0.01 us -> 62.2 us  [body(): lax.all_to_all(send_grads, 'expert', split_axis=0, concat_axis=0, tiled=T...]
    all_gather x1 -> x0, blocking collectives: 22.5 us -> none  [body(): lax.all_gather(down_weight, 'dp', axis=2, tiled=True)]
    all_to_all x1, waiting for transfers between devices: 59.5 us -> 72.4 us  [body(): lax.all_to_all(send_inputs, 'expert', split_axis=0, concat_axis=0, tiled=...]
    all_to_all x0 -> x1, starting transfers between devices: none -> 10.2 us  [body(): lax.all_to_all(jnp.stack([down_weight] * lax.axis_size('dp')), 'dp', 0, 0)]
    all_to_all x1, starting transfers between devices: 23.6 us -> 16.3 us  [body(): lax.all_to_all(d_rows.reshape(experts, capacity, model_width), 'expert',...]
    all_gather x1, blocking collectives: 30.3 us -> 37.3 us  [body(): lax.all_gather(gate_weight, 'dp', axis=1, tiled=True)]
    all_to_all x1, starting transfers between devices: 11.8 us -> 6.25 us  [body(): lax.all_to_all(send_inputs, 'expert', split_axis=0, concat_axis=0, tiled=...]
    all_to_all x1, starting transfers between devices: 6.25 us -> 11.6 us  [body(): lax.all_to_all(send_grads, 'expert', split_axis=0, concat_axis=0, tiled=T...]
  transfers between devices with their start and end apart: 4 -> 5, of which waited for: 2 -> 3; matrix products, arithmetic and copies ran while one was open for 12% -> 10% of each run, Pallas kernels for 0% -> 0%
where the time goes in v1:
time: 395 us; the launch traced here: 394 us
  waiting for transfers between devices  204 us (52%)
  blocking collectives  60.8 us (15%)
  starting transfers between devices  44.6 us (11%)
  local copies, waits for them, and re-layouts  40.6 us (10%)
  other arithmetic  15 us (4%)
  matrix products  15 us (4%)
  between operations  14.2 us (4%)
    all_to_all x1, waiting for transfers between devices, body(): lax.all_to_all(send_inputs, 'expert', split_axis=0, concat_axis=0, tiled=...  72.4 us
    all_to_all x1, waiting for transfers between devices, body(): lax.all_to_all(d_rows.reshape(experts, capacity, model_width), 'expert',...  68.9 us
    all_to_all x1, waiting for transfers between devices, body(): lax.all_to_all(send_grads, 'expert', split_axis=0, concat_axis=0, tiled=T...  62.2 us
    all_gather x1, blocking collectives, body(): lax.all_gather(gate_weight, 'dp', axis=1, tiled=True)  37.3 us
    all_gather x1, blocking collectives, body(): lax.all_gather(up_weight, 'dp', axis=1, tiled=True)  23.6 us
    all_to_all x1, starting transfers between devices, body(): lax.all_to_all(d_rows.reshape(experts, capacity, model_width), 'expert',...  16.3 us
    all_to_all x1, starting transfers between devices, body(): lax.all_to_all(send_grads, 'expert', split_axis=0, concat_axis=0, tiled=T...  11.6 us
    all_to_all x1, starting transfers between devices, body(): lax.all_to_all(jnp.stack([down_weight] * lax.axis_size('dp')), 'dp', 0, 0)  10.2 us
  transfers between devices with their start and end apart: 5, of which 3 were waited for; matrix products, arithmetic and copies ran while one was open for 10% of the time, Pallas kernels for 0%

profile of v1, /device:TPU:1, one launch (start us, length us, event | category | flops | bytes accessed | tf_op | source)
XLA Modules:
  0.0 393.8 jit_solution(10095301421623919974)
XLA Ops:
  11.7 6.4 %scatter_custom_fusion = bf16[1152,1024]{1,0:T(8,128)(2,1)S(1)} fusion(s32[1024]{0:T(1024)S(1)} %bitcast.40, f32[128,1024]{1,0:T(8,128)S(1)} %convert_element_type.34, f32[1024]{0:T(1024)S(1)} %mul.60, bf16[]{:T(256)} %constant.6.clone.1), kind=kCustom, calls=%fused_computation.7 | custom fusion | flops 2097152 | bytes 2887682 | tf_op jit(solution)/shard_map/scatter | solution.py:59
  18.1 2.4 reshape.79
  20.5 11.6 %all-to-all-start = ((bf16[64,18,1024]{2,1,0:T(8,128)(2,1)}), bf16[64,18,1024]{2,1,0:T(8,128)(2,1)S(1)}, u32[]{:S(2)}, u32[]{:S(2)}) async-start(bf16[64,18,1024]{2,1,0:T(8,128)(2,1)} %reshape.79), calls=%async_computation | async-start | bytes 6291456 | tf_op jit(solution)/shard_map/all_to_all | solution.py:74
  32.2 7.0 %scatter_custom_fusion.1 = bf16[1152,1024]{1,0:T(8,128)(2,1)} fusion(s32[1024]{0:T(1024)S(1)} %bitcast.41, bf16[]{:T(256)} %constant.6.clone.1, bf16[128,1024]{1,0:T(8,128)(2,1)S(1)} %copy-done), kind=kCustom, calls=%fused_computation.9 | custom fusion | bytes 2621442 | tf_op jit(solution)/shard_map/scatter | solution.py:53
  39.2 4.3 %reshape.83 = bf16[64,18,1024]{2,1,0:T(8,128)(2,1)} reshape(bf16[1152,1024]{1,0:T(8,128)(2,1)} %scatter_custom_fusion.1) | data formatting | bytes 4718592 | tf_op jit(solution)/shard_map/reshape | solution.py:54
  43.5 62.2 %all-to-all-done = bf16[64,18,1024]{2,1,0:T(8,128)(2,1)S(1)} async-done(((bf16[64,18,1024]{2,1,0:T(8,128)(2,1)}), bf16[64,18,1024]{2,1,0:T(8,128)(2,1)S(1)}, u32[]{:S(2)}, u32[]{:S(2)}) %all-to-all-start) | async-done | bytes 2359328 | tf_op jit(solution)/shard_map/all_to_all | solution.py:74
  105.7 6.2 %all-to-all-start.2 = ((bf16[64,18,1024]{2,1,0:T(8,128)(2,1)}), bf16[64,18,1024]{2,1,0:T(8,128)(2,1)}, u32[]{:S(2)}, u32[]{:S(2)}) async-start(bf16[64,18,1024]{2,1,0:T(8,128)(2,1)} %reshape.83), calls=%async_computation.2 | async-start | bytes 6291456 | tf_op jit(solution)/shard_map/all_to_all | solution.py:73
  112.9 72.4 %all-to-all-done.2 = bf16[64,18,1024]{2,1,0:T(8,128)(2,1)} async-done(((bf16[64,18,1024]{2,1,0:T(8,128)(2,1)}), bf16[64,18,1024]{2,1,0:T(8,128)(2,1)}, u32[]{:S(2)}, u32[]{:S(2)}) %all-to-all-start.2) | async-done | bytes 2359328 | tf_op jit(solution)/shard_map/all_to_all | solution.py:73
  186.3 10.2 %all-to-all-start.1 = ((bf16[8,1,384,128]{2,3,1,0:T(8,128)(2,1)}), bf16[8,1,384,128]{2,3,1,0:T(8,128)(2,1)}, u32[]{:S(2)}, u32[]{:S(2)}) async-start(bf16[8,1,384,128]{2,3,1,0:T(8,128)(2,1)} %stack.2), calls=%async_computation.1 | async-start | bytes 1572864 | tf_op jit(solution)/shard_map/all_to_all | solution.py:66
  196.5 37.3 %all_gather.6 = bf16[1,1024,384]{2,1,0:T(8,128)(2,1)} all-gather(bf16[1,128,384]{2,1,0:T(8,128)(2,1)} %param.11), channel_id=1, replica_groups=mesh['dp'=8,'expert'=64] {'dp'}, dimensions={1}, use_global_device_ids=true | all-gather | bytes 884736 | tf_op jit(solution)/shard_map/all_gather | solution.py:63
  233.8 23.6 %all_gather.7 = bf16[1,1024,384]{2,1,0:T(8,128)(2,1)} all-gather(bf16[1,128,384]{2,1,0:T(8,128)(2,1)S(1)} %copy-done.5), channel_id=1, replica_groups=mesh['dp'=8,'expert'=64] {'dp'}, dimensions={1}, use_global_device_ids=true | all-gather | bytes 884736 | tf_op jit(solution)/shard_map/all_gather | solution.py:64
  257.3 2.3 reshape.80
  259.6 3.0 reshape.84
  262.6 3.5 fusion.10
  269.2 4.7 %multiply_convert_fusion.2 = (bf16[1152,384]{0,1:T(8,128)(2,1)S(1)}, bf16[1152,384]{0,1:T(8,128)(2,1)S(1)}) fusion(f32[1152,768]{0,1:T(8,128)} %copy-done.6, bf16[1152,1024]{1,0:T(8,128)(2,1)} %reshape.80, bf16[384,1024]{0,1:T(8,128)(2,1)} %bitcast.5), kind=kOutput, calls=%fused_computation.16 | convolution fusion | flops 911720448 | bytes 8454144 | tf_op jit(solution)/shard_map/dot_general | solution.py:27
  273.9 3.3 convolution_convert_fusion.1
  277.2 2.1 convolution_convert_fusion
  279.3 2.4 reshape.85
  281.7 16.3 %all-to-all-start.3 = ((bf16[64,18,1024]{2,1,0:T(8,128)(2,1)}), bf16[64,18,1024]{2,1,0:T(8,128)(2,1)}, u32[]{:S(2)}, u32[]{:S(2)}) async-start(bf16[64,18,1024]{2,1,0:T(8,128)(2,1)} %reshape.85), calls=%async_computation.3 | async-start | bytes 6291456 | tf_op jit(solution)/shard_map/all_to_all | solution.py:79
  299.8 2.6 copy.36
  302.5 68.9 %all-to-all-done.3 = bf16[64,18,1024]{2,1,0:T(8,128)(2,1)} async-done(((bf16[64,18,1024]{2,1,0:T(8,128)(2,1)}), bf16[64,18,1024]{2,1,0:T(8,128)(2,1)}, u32[]{:S(2)}, u32[]{:S(2)}) %all-to-all-start.3) | async-done | bytes 2359328 | tf_op jit(solution)/shard_map/all_to_all | solution.py:79
  371.4 2.9 reshape.86
  374.3 5.3 %gather_fusion = bf16[1024,1024]{1,0:T(8,128)(2,1)} fusion(bf16[1152,1024]{1,0:T(8,128)(2,1)S(1)} %reshape.86, s32[1024]{0:T(1024)S(1)} %broadcast_clamp_fusion), kind=kCustom, calls=%fused_computation | custom fusion | bytes 4198400 | tf_op jit(solution)/shard_map/gather | solution.py:86
  379.7 3.7 bitcast_reduce_fusion
  (39 shorter events, 14.9 us)
Async XLA Ops:
  7.2 25.0 %copy-start = (bf16[128,1024]{1,0:T(8,128)(2,1)S(1)}, bf16[128,1024]{1,0:T(8,128)(2,1)}, u32[]{:S(2)}) copy-start(bf16[128,1024]{1,0:T(8,128)(2,1)} %param.7) | copy-start | bytes 786436
  20.5 85.1 %all-to-all-start = ((bf16[64,18,1024]{2,1,0:T(8,128)(2,1)}), bf16[64,18,1024]{2,1,0:T(8,128)(2,1)S(1)}, u32[]{:S(2)}, u32[]{:S(2)}) async-start(bf16[64,18,1024]{2,1,0:T(8,128)(2,1)} %reshape.79), calls=%async_computation | async-start | bytes 6291456 | tf_op jit(solution)/shard_map/all_to_all | solution.py:74
  105.7 79.7 %all-to-all-start.2 = ((bf16[64,18,1024]{2,1,0:T(8,128)(2,1)}), bf16[64,18,1024]{2,1,0:T(8,128)(2,1)}, u32[]{:S(2)}, u32[]{:S(2)}) async-start(bf16[64,18,1024]{2,1,0:T(8,128)(2,1)} %reshape.83), calls=%async_computation.2 | async-start | bytes 6291456 | tf_op jit(solution)/shard_map/all_to_all | solution.py:73
  186.3 47.4 %copy-start.5 = (bf16[1,128,384]{2,1,0:T(8,128)(2,1)S(1)}, bf16[1,128,384]{2,1,0:T(8,128)(2,1)}, u32[]{:S(2)}) copy-start(bf16[1,128,384]{2,1,0:T(8,128)(2,1)} %param.12) | copy-start | bytes 294916
  186.3 82.8 %all-to-all-start.1 = ((bf16[8,1,384,128]{2,3,1,0:T(8,128)(2,1)}), bf16[8,1,384,128]{2,3,1,0:T(8,128)(2,1)}, u32[]{:S(2)}, u32[]{:S(2)}) async-start(bf16[8,1,384,128]{2,3,1,0:T(8,128)(2,1)} %stack.2), calls=%async_computation.1 | async-start | bytes 1572864 | tf_op jit(solution)/shard_map/all_to_all | solution.py:66
  259.6 3.0 copy-start.2
  262.6 5.3 %copy-start.1 = (bf16[1152,1024]{1,0:T(8,128)(2,1)S(1)}, bf16[1152,1024]{1,0:T(8,128)(2,1)}, u32[]{:S(2)}) copy-start(bf16[1152,1024]{1,0:T(8,128)(2,1)} %reshape.80) | copy-start | bytes 7077892
  266.2 1.8 copy-start.6
  273.8 3.4 copy-start.3
  273.8 3.4 copy-start.4
  281.7 89.7 %all-to-all-start.3 = ((bf16[64,18,1024]{2,1,0:T(8,128)(2,1)}), bf16[64,18,1024]{2,1,0:T(8,128)(2,1)}, u32[]{:S(2)}, u32[]{:S(2)}) async-start(bf16[64,18,1024]{2,1,0:T(8,128)(2,1)} %reshape.85), calls=%async_computation.3 | async-start | bytes 6291456 | tf_op jit(solution)/shard_map/all_to_all | solution.py:79
  297.9 85.5 %reduce-scatter.4.cloned.1.call-start = ((), (), s32[]{:S(2)}) async-start(), calls=%async_computation.5 | async-start | bytes 2654208
Sparse Core Ops, SparseCore 0:
  302.6 42.2 reduce-scatter.3
